TPU v7x, 32 devices: a whole 2x2x4 slice. The times are simulated.
32 devices in a mesh: dp: 8 (over y, x, core), tensor: 4 (over z).
Axes of the slice: x: 2, y: 2, z: 4, core: 2. Of those that a mesh axis runs over, the one named last changes fastest.
Arguments:
- tokens: bfloat16 [3072, 8192], P('dp', 'tensor'), may hold values from -6 to 6
- up_first: bfloat16 [16, 512, 512], P('tensor'), may hold values from -0.25 to 0.25
- up_second: bfloat16 [16, 512, 2048], P('tensor'), may hold values from -0.25 to 0.25
- down_first: bfloat16 [16, 2048, 512], P('tensor'), may hold values from -0.125 to 0.125
- down_second: bfloat16 [16, 512, 512], P('tensor'), may hold values from -0.25 to 0.25
- cotangent: bfloat16 [3072, 8192], P('dp', 'tensor'), may hold values from -6 to 6
Outputs:
- layer_out: bfloat16 [3072, 8192], P('dp', 'tensor')
- grad_tokens: bfloat16 [3072, 8192], P('dp', 'tensor')
- grad_up_first: float32 [16, 512, 512], P('tensor', 'dp')
- grad_up_second: float32 [16, 512, 2048], P('tensor', 'dp')
- grad_down_first: float32 [16, 2048, 512], P('tensor', 'dp')
- grad_down_second: float32 [16, 512, 512], P('tensor', 'dp')
All inputs are finite; a program needn't handle non-finite values.
Results may differ from a plain program's by a relative error of at most 0.023.
Values may be sent and summed in bfloat16 or wider, within the bound.
No kernel may reach another device: no remote copies, remote signals or barrier semaphores. Data moves between devices by JAX's collectives and lax.ppermute only.
A program may use at most 128 MiB of HBM per device.

v0:
```python
import jax
import jax.numpy as jnp
from jax import lax
from jax.sharding import PartitionSpec as P

NB = 16
gelu_coeff = 0.7978845608028654
cubic_coeff = 0.044715


def gelu_pair(hidden):
    inner_arg = gelu_coeff * (hidden + cubic_coeff * hidden * hidden * hidden)
    tangent = jnp.tanh(inner_arg)
    gelu_value = 0.5 * hidden * (1.0 + tangent)
    gelu_slope = 0.5 * (1.0 + tangent) + 0.5 * hidden * (1.0 - tangent * tangent) * gelu_coeff * (
        1.0 + 3.0 * cubic_coeff * hidden * hidden
    )
    return (gelu_value, gelu_slope)


def regroup(sliced, apply_fn):
    return apply_fn(lax.all_to_all(sliced, "tensor", split_axis=2, concat_axis=0, tiled=True))


def body(tokens, up_first, up_second, down_first, down_second, cotangent):
    token_rows = tokens.shape[0]
    local_blocks = up_first.shape[0]
    block_size = up_first.shape[1]
    hidden_size = up_second.shape[2]
    slice_width = block_size // NB
    data_count = lax.axis_size("dp")
    grad_scale = (token_rows * data_count) ** (-0.5)
    x_three = tokens.reshape(token_rows, local_blocks, block_size)
    up_four = up_first.reshape(local_blocks, block_size, NB, slice_width)
    mixed_up = jnp.einsum(
        "tbi,bijc->bcjt", x_three, up_four, preferred_element_type=jnp.float32
    ).astype(jnp.bfloat16)

    def lift_up(received):
        regrouped = received.reshape(block_size, local_blocks, received.shape[3])
        return (
            regrouped,
            jnp.einsum("mjt,jmo->jot", regrouped, up_second, preferred_element_type=jnp.float32),
        )

    regrouped_up, pre_act = regroup(mixed_up, lift_up)
    gelu_value, gelu_slope = gelu_pair(pre_act)
    activated = gelu_value.astype(jnp.bfloat16)
    down_four = down_first.reshape(local_blocks, hidden_size, NB, slice_width)
    mixed_down = jnp.einsum(
        "jmt,jmkc->jckt", activated, down_four, preferred_element_type=jnp.float32
    ).astype(jnp.bfloat16)

    def settle(received):
        regrouped = received.reshape(block_size, local_blocks, received.shape[3])
        return (
            regrouped,
            jnp.einsum("mkt,kmo->kot", regrouped, down_second, preferred_element_type=jnp.float32),
        )

    regrouped_down, branch = regroup(mixed_down, settle)
    branch_rows = branch.transpose(2, 0, 1).reshape(token_rows, local_blocks * block_size)
    layer_out = (tokens.astype(jnp.float32) + branch_rows).astype(jnp.bfloat16)
    grad_three = cotangent.reshape(token_rows, local_blocks, block_size)
    last_four = down_second.reshape(local_blocks, NB, slice_width, block_size)
    back_down = jnp.einsum(
        "tko,kjco->kcjt", grad_three, last_four, preferred_element_type=jnp.float32
    ).astype(jnp.bfloat16)

    def descend(received):
        regrouped = received.reshape(block_size, local_blocks, received.shape[3])
        return (
            regrouped,
            jnp.einsum("ojt,jmo->jmt", regrouped, down_first, preferred_element_type=jnp.float32),
        )

    grad_mid, grad_act = regroup(back_down, descend)
    grad_pre = (grad_act * gelu_slope).astype(jnp.bfloat16)
    term_fourth = grad_scale * jnp.einsum(
        "mkt,tko->mko", regrouped_down, grad_three, preferred_element_type=jnp.float32
    )
    term_third = grad_scale * jnp.einsum(
        "jmt,ojt->mjo", activated, grad_mid, preferred_element_type=jnp.float32
    )
    up_back = up_second.reshape(local_blocks, NB, slice_width, hidden_size)
    back_up = jnp.einsum(
        "jot,jbco->jcbt", grad_pre, up_back, preferred_element_type=jnp.float32
    ).astype(jnp.bfloat16)

    def arrive(received):
        regrouped = received.reshape(block_size, local_blocks, received.shape[3])
        return (
            regrouped,
            jnp.einsum("obt,bio->bit", regrouped, up_first, preferred_element_type=jnp.float32),
        )

    grad_in, back_branch = regroup(back_up, arrive)
    back_rows = back_branch.transpose(2, 0, 1).reshape(token_rows, local_blocks * block_size)
    grad_tokens = (cotangent.astype(jnp.float32) + back_rows).astype(jnp.bfloat16)
    term_second = grad_scale * jnp.einsum(
        "mjt,jot->mjo", regrouped_up, grad_pre, preferred_element_type=jnp.float32
    )
    term_first = grad_scale * jnp.einsum(
        "tbi,obt->ibo", x_three, grad_in, preferred_element_type=jnp.float32
    )
    sum_first, sum_second, sum_third, sum_fourth = (
        lax.psum_scatter(
            term_first.astype(jnp.bfloat16), "dp", scatter_dimension=0, tiled=True
        ).astype(jnp.float32),
        lax.psum_scatter(
            term_second.astype(jnp.bfloat16), "dp", scatter_dimension=0, tiled=True
        ).astype(jnp.float32),
        lax.psum_scatter(
            term_third.astype(jnp.bfloat16), "dp", scatter_dimension=0, tiled=True
        ).astype(jnp.float32),
        lax.psum_scatter(
            term_fourth.astype(jnp.bfloat16), "dp", scatter_dimension=0, tiled=True
        ).astype(jnp.float32),
    )
    grad_up_first = sum_first.transpose(1, 0, 2)
    grad_up_second = sum_second.transpose(1, 0, 2)
    grad_down_first = sum_third.transpose(1, 0, 2)
    grad_down_second = sum_fourth.transpose(1, 0, 2)
    return (
        layer_out,
        grad_tokens,
        grad_up_first,
        grad_up_second,
        grad_down_first,
        grad_down_second,
    )


def solution(mesh):
    in_specs = (
        P("dp", "tensor"),
        P("tensor", None, None),
        P("tensor", None, None),
        P("tensor", None, None),
        P("tensor", None, None),
        P("dp", "tensor"),
    )
    out_specs = (
        P("dp", "tensor"),
        P("dp", "tensor"),
        P("tensor", "dp", None),
        P("tensor", "dp", None),
        P("tensor", "dp", None),
        P("tensor", "dp", None),
    )
    return jax.shard_map(body, mesh=mesh, in_specs=in_specs, out_specs=out_specs, check_vma=False)
```

profile of v0, /device:TPU:0, one launch (start us, length us, event | category | flops | bytes accessed | tf_op | source)
XLA Modules:
  0.0 465.9 jit_solution(12066908594046687807)
XLA Ops:
  7.2 4.0 reshape.59
  15.3 6.3 %all-to-all-start.2 = ((bf16[4,32,16,384]{3,1,0,2:T(8,128)(2,1)}), bf16[4,32,16,384]{3,1,0,2:T(8,128)(2,1)}, u32[]{:S(2)}, u32[]{:S(2)}) async-start(bf16[4,32,16,384]{3,1,0,2:T(8,128)(2,1)} %copy.105), calls=%async_computation.2 | async-start | bytes 3145728 | tf_op jit(solution)/shard_map/all_to_all | solution.py:22
  25.4 4.1 copy.90
  34.3 24.4 %all-to-all-done.2 = bf16[4,32,16,384]{3,1,0,2:T(8,128)(2,1)} async-done(((bf16[4,32,16,384]{3,1,0,2:T(8,128)(2,1)}), bf16[4,32,16,384]{3,1,0,2:T(8,128)(2,1)}, u32[]{:S(2)}, u32[]{:S(2)}) %all-to-all-start.2) | async-done | bytes 1572896 | tf_op jit(solution)/shard_map/all_to_all | solution.py:22
  58.7 4.4 all-to-all-start
  65.8 33.7 %all-to-all-done = bf16[4,32,16,384]{3,1,0,2:T(8,128)(2,1)} async-done(((bf16[4,32,16,384]{3,1,0,2:T(8,128)(2,1)}), bf16[4,32,16,384]{3,1,0,2:T(8,128)(2,1)}, u32[]{:S(2)}, u32[]{:S(2)}) %all-to-all-start) | async-done | bytes 1572896 | tf_op jit(solution)/shard_map/all_to_all | solution.py:22
  102.3 6.0 %fusion.34 = f32[4,384,2048]{2,1,0:T(8,128)S(1)} fusion(bf16[512,4,384]{2,0,1:T(8,128)(2,1)S(1)} %bitcast.120, bf16[4,512,2048]{2,1,0:T(8,128)(2,1)} %param.8), kind=kOutput, calls=%fused_computation.45 | convolution fusion | flops 3221225472 | bytes 22544384 | tf_op jit(solution)/shard_map/mjt,jmo->jot/dot_general | solution.py:43
  108.3 11.5 %fusion.33 = f32[4,384,512]{1,2,0:S(1)} fusion(bf16[4,2048,512]{2,1,0:T(8,128)(2,1)} %param.9, f32[4,384,2048]{2,1,0:T(8,128)S(1)} %fusion.34), kind=kOutput, calls=%fused_computation.44 | convolution fusion | flops 3249537024 | bytes 24117248
  121.4 4.3 all-to-all-start.1
  126.3 16.0 %fusion.6 = bf16[4,2048,384]{1,2,0:T(8,128)(2,1)} fusion(f32[4,384,2048]{2,1,0:T(8,128)} %copy-done.1, bf16[512,4,384]{2,0,1:T(8,128)(2,1)} %bitcast.124, bf16[4,2048,512]{2,1,0:T(8,128)(2,1)} %param.9), kind=kOutput, calls=%fused_computation.10 | convolution fusion | flops 3280994304 | bytes 28835840 | tf_op jit(solution)/shard_map/ojt,jmo->jmt/dot_general | solution.py:74
  142.3 20.0 %all-to-all-done.1 = bf16[4,32,16,384]{3,1,0,2:T(8,128)(2,1)} async-done(((bf16[4,32,16,384]{3,1,0,2:T(8,128)(2,1)}), bf16[4,32,16,384]{3,1,0,2:T(8,128)(2,1)}, u32[]{:S(2)}, u32[]{:S(2)}) %all-to-all-start.1) | async-done | bytes 1572896 | tf_op jit(solution)/shard_map/all_to_all | solution.py:22
  167.7 9.9 %fusion.24 = bf16[4,32,16,384]{3,1,2,0:T(8,128)(2,1)S(1)} fusion(bf16[4,16,32,2048]{3,2,1,0:T(8,128)(2,1)} %bitcast.113, bf16[4,2048,384]{1,2,0:T(8,128)(2,1)} %fusion.6), kind=kOutput, calls=%fused_computation.39 | convolution fusion | flops 3222011904 | bytes 16252928 | tf_op jit(solution)/shard_map/jot,jbco->jcbt/dot_general | solution.py:86
  179.0 4.4 all-to-all-start.3
  183.6 11.6 %fusion.7 = bf16[512,4,2048]{0,2,1:T(8,128)(2,1)} fusion(bf16[4,2048,384]{1,2,0:T(8,128)(2,1)} %fusion.6, bf16[512,4,384]{2,0,1:T(8,128)(2,1)} %bitcast.121), kind=kOutput, calls=%fused_computation.13 | convolution fusion | flops 3229614080 | bytes 16252928 | tf_op jit(solution)/shard_map/mjt,jot->mjo/dot_general | solution.py:100
  195.2 14.9 %copy.118 = bf16[512,4,2048]{2,1,0:T(4,128)(2,1)} copy(bf16[512,4,2048]{0,2,1:T(8,128)(2,1)} %fusion.7) | data formatting | bytes 16777216 | tf_op jit(solution)/shard_map/convert_element_type | solution.py:111
  210.1 9.6 %all-to-all-done.3 = bf16[4,32,16,384]{3,1,0,2:T(8,128)(2,1)} async-done(((bf16[4,32,16,384]{3,1,0,2:T(8,128)(2,1)}), bf16[4,32,16,384]{3,1,0,2:T(8,128)(2,1)}, u32[]{:S(2)}, u32[]{:S(2)}) %all-to-all-start.3) | async-done | bytes 1572896 | tf_op jit(solution)/shard_map/all_to_all | solution.py:22
  225.2 4.5 copy.116
  229.9 11.0 %fusion.8 = bf16[2048,4,512]{0,2,1:T(8,128)(2,1)} fusion(bf16[512,4,384]{2,0,1:T(8,128)(2,1)} %bitcast.125, f32[4,384,2048]{2,1,0:T(8,128)} %copy-done.1), kind=kOutput, calls=%fused_computation.14 | convolution fusion | flops 3257925632 | bytes 22544384 | tf_op jit(solution)/shard_map/jmt,ojt->mjo/dot_general | solution.py:82
  247.4 4.1 convolution_bitcast_fusion.1
  255.1 4.1 fusion.12
  261.9 4.9 %convolution_bitcast_fusion = f32[384,4,512]{2,0,1:T(8,128)} fusion(bf16[512,4,384]{2,0,1:T(8,128)(2,1)} %bitcast.119, bf16[4,512,512]{2,1,0:T(8,128)(2,1)} %param.7), kind=kOutput, calls=%fused_computation.25 | convolution fusion | flops 805306368 | bytes 6815744 | tf_op jit(solution)/shard_map/obt,bio->bit/dot_general | solution.py:94
  270.5 3.9 fusion.11
  278.9 99.8 %all-reduce.5.cloned.1.call-done = (bf16[512,4,512]{2,1,0:T(4,128)(2,1)}, bf16[512,4,2048]{2,1,0:T(4,128)(2,1)}) async-done(((bf16[512,4,512]{2,1,0:T(4,128)(2,1)}, bf16[512,4,2048]{2,1,0:T(4,128)(2,1)}), (bf16[512,4,512]{2,1,0:T(4,128)(2,1)}, bf16[512,4,2048]{2,1,0:T(4,128)(2,1)})) %all-reduce.5.cloned.1.call-update) | async-done | bytes 10485776
  384.6 69.0 %reduce-scatter.3.cloned.1.call-done = bf16[256,4,512]{0,2,1:T(8,128)(2,1)} async-done(((bf16[2048,4,512]{0,2,1:T(8,128)(2,1)}), bf16[256,4,512]{0,2,1:T(8,128)(2,1)}) %reduce-scatter.3.cloned.1.call-update) | async-done | bytes 1048592 | tf_op jit(solution)/shard_map/reduce_scatter | solution.py:113
  (51 shorter events, 64.8 us)
Async XLA Ops:
  7.2 4.0 copy-start
  15.3 43.4 %all-to-all-start.2 = ((bf16[4,32,16,384]{3,1,0,2:T(8,128)(2,1)}), bf16[4,32,16,384]{3,1,0,2:T(8,128)(2,1)}, u32[]{:S(2)}, u32[]{:S(2)}) async-start(bf16[4,32,16,384]{3,1,0,2:T(8,128)(2,1)} %copy.105), calls=%async_computation.2 | async-start | bytes 3145728 | tf_op jit(solution)/shard_map/all_to_all | solution.py:22
  58.7 40.9 %all-to-all-start = ((bf16[4,32,16,384]{3,1,0,2:T(8,128)(2,1)}), bf16[4,32,16,384]{3,1,0,2:T(8,128)(2,1)}, u32[]{:S(2)}, u32[]{:S(2)}) async-start(bf16[4,32,16,384]{3,1,0,2:T(8,128)(2,1)} %copy.92), calls=%async_computation | async-start | bytes 3145728 | tf_op jit(solution)/shard_map/all_to_all | solution.py:22
  101.2 1.1 copy-start.6
  108.3 11.5 %copy-start.1 = (f32[4,384,2048]{2,1,0:T(8,128)}, f32[4,384,2048]{2,1,0:T(8,128)S(1)}, u32[]{:S(2)}) copy-start(f32[4,384,2048]{2,1,0:T(8,128)S(1)} %fusion.34) | copy-start | bytes 37748740
  121.4 40.9 %all-to-all-start.1 = ((bf16[4,32,16,384]{3,1,0,2:T(8,128)(2,1)}), bf16[4,32,16,384]{3,1,0,2:T(8,128)(2,1)}, u32[]{:S(2)}, u32[]{:S(2)}) async-start(bf16[4,32,16,384]{3,1,0,2:T(8,128)(2,1)} %copy.98), calls=%async_computation.1 | async-start | bytes 3145728 | tf_op jit(solution)/shard_map/all_to_all | solution.py:22
  125.8 151.3 %reduce-scatter.5.cloned.1.call-start = ((), (), s32[]{:S(2)}) async-start(), calls=%async_computation.7 | async-start | bytes 2359296 | tf_op jit(solution)/shard_map/reduce_scatter | solution.py:116
  162.3 2.8 copy-start.3
  164.0 1.1 copy-start.4
  179.0 40.7 %all-to-all-start.3 = ((bf16[4,32,16,384]{3,1,0,2:T(8,128)(2,1)}), bf16[4,32,16,384]{3,1,0,2:T(8,128)(2,1)}, u32[]{:S(2)}, u32[]{:S(2)}) async-start(bf16[4,32,16,384]{3,1,0,2:T(8,128)(2,1)} %copy.110), calls=%async_computation.3 | async-start | bytes 3145728 | tf_op jit(solution)/shard_map/all_to_all | solution.py:22
  183.4 195.3 %all-reduce.5.cloned.1.call-start = ((), (), s32[]{:S(2)}) async-start(), calls=%async_computation.8 | async-start | bytes 20971520
  219.7 2.9 copy-start.2
  221.4 1.2 copy-start.5
  229.7 223.9 %reduce-scatter.3.cloned.1.call-start = ((), (), s32[]{:S(2)}) async-start(), calls=%async_computation.6 | async-start | bytes 9437184 | tf_op jit(solution)/shard_map/reduce_scatter | solution.py:113
  241.0 5.2 %copy-start.7 = (u32[32]{0:T(128)S(1)}, u32[32]{0:T(128)}, u32[]{:S(2)}) copy-start(u32[32]{0:T(128)} %constant.16) | copy-start | bytes 388
Sparse Core Ops, SparseCore 0:
  167.8 40.3 reduce-scatter.4
  229.8 148.8 all-reduce.4
  382.1 71.3 reduce-scatter.2
where the time goes:
time: 474 us; the launch traced here: 466 us
  waiting for transfers between devices  257 us (54%)
  matrix products  86 us (18%)
  local copies, waits for them, and re-layouts  73 us (15%)
  starting transfers between devices  20.3 us (4%)
  other arithmetic  15.2 us (3%)
  between operations  14.8 us (3%)
    unnamed x4, waiting for transfers between devices  99.8 us
    all_to_all x4, waiting for transfers between devices, regroup(): lax.all_to_all(sliced, 'tensor', split_axis=2, concat_axis=0, tiled=True)  87.7 us
    reduce_scatter x1, waiting for transfers between devices, body(): lax.psum_scatter(term_third.astype(jnp.bfloat16), 'dp', scatter_dimension...  69 us
    unnamed x25, local copies, waits for them, and re-layouts  25.1 us
    all_to_all x4, starting transfers between devices, regroup(): lax.all_to_all(sliced, 'tensor', split_axis=2, concat_axis=0, tiled=True)  19.4 us
    dot_general x1, matrix products, descend(): jnp.einsum('ojt,jmo->jmt', regrouped, down_first, preferred_element_type=...  16 us
    convert_element_type x1, local copies, waits for them, and re-layouts, body(): term_second.astype(jnp.bfloat16)  14.9 us
    dot_general x1, matrix products, body(): jnp.einsum('mjt,jot->mjo', regrouped_up, grad_pre, preferred_element_type...  11.6 us
  transfers between devices with their start and end apart: 7, of which 6 were waited for; matrix products, arithmetic and copies ran while one was open for 28% of the time, Pallas kernels for 0%

commit v1 on v0

--- a/solution.py
+++ b/solution.py
@@ -19,7 +19,14 @@
 
 
 def regroup(sliced, apply_fn):
-    return apply_fn(lax.all_to_all(sliced, "tensor", split_axis=2, concat_axis=0, tiled=True))
+    return apply_fn(
+        jnp.concatenate(
+            lax.all_to_all(
+                jnp.stack(jnp.split(sliced, lax.axis_size("tensor"), axis=2)), "tensor", 0, 0
+            ),
+            axis=0,
+        )
+    )
 
 
 def body(tokens, up_first, up_second, down_first, down_second, cotangent):

time: 474 us -> 458 us (0.966)
  waiting for transfers between devices: 257 us -> 237 us
  other arithmetic: 15.2 us -> 20.8 us
    all_to_all x4, waiting for transfers between devices: 87.7 us -> 68.5 us  [regroup(): lax.all_to_all(jnp.stack(jnp.split(sliced, lax.axis_size('tensor'), axis=...]
    convert_element_type x4 -> x0, local copies, waits for them, and re-layouts: 5.58 us -> none  [the longest x1 1.41 us: body(): mixed_down = jnp.einsum('jmt,jmkc->jckt', activated, down_four, preferred...]
    another operation x0 -> x4, other arithmetic: none -> 5.55 us  [regroup(): jnp.stack(jnp.split(sliced, lax.axis_size('tensor'), axis=2))]
    unnamed x25 -> x27, local copies, waits for them, and re-layouts: 25.1 us -> 26.2 us
  transfers between devices with their start and end apart: 7 -> 7, of which waited for: 6 -> 6; matrix products, arithmetic and copies ran while one was open for 28% -> 33% of each run, Pallas kernels for 0% -> 0%
where the time goes in v1:
time: 458 us; the launch traced here: 449 us
  waiting for transfers between devices  237 us (52%)
  matrix products  87.6 us (19%)
  local copies, waits for them, and re-layouts  68.3 us (15%)
  other arithmetic  20.8 us (5%)
  starting transfers between devices  20.4 us (4%)
  between operations  14.9 us (3%)
    unnamed x4, waiting for transfers between devices  99.9 us
    reduce_scatter x1, waiting for transfers between devices, body(): lax.psum_scatter(term_third.astype(jnp.bfloat16), 'dp', scatter_dimension...  69 us
    all_to_all x4, waiting for transfers between devices, regroup(): lax.all_to_all(jnp.stack(jnp.split(sliced, lax.axis_size('tensor'), axis=...  68.5 us
    unnamed x27, local copies, waits for them, and re-layouts  26.2 us
    all_to_all x4, starting transfers between devices, regroup(): lax.all_to_all(jnp.stack(jnp.split(sliced, lax.axis_size('tensor'), axis=...  19.4 us
    dot_general x1, matrix products, descend(): jnp.einsum('ojt,jmo->jmt', regrouped, down_first, preferred_element_type=...  17.6 us
    convert_element_type x1, local copies, waits for them, and re-layouts, body(): term_second.astype(jnp.bfloat16)  14.9 us
    dot_general x1, matrix products, body(): jnp.einsum('mjt,jot->mjo', regrouped_up, grad_pre, preferred_element_type...  11.5 us
  transfers between devices with their start and end apart: 7, of which 6 were waited for; matrix products, arithmetic and copies ran while one was open for 33% of the time, Pallas kernels for 0%

profile of v1, /device:TPU:0, one launch (start us, length us, event | category | flops | bytes accessed | tf_op | source)
XLA Modules:
  0.0 449.3 jit_solution(3907767843011793881)
XLA Ops:
  7.2 4.0 reshape.37
  11.2 4.1 copy.57
  20.3 6.3 %all-to-all-start = ((bf16[4,4,32,4,384]{4,2,3,1,0:T(8,128)(2,1)}), bf16[4,4,32,4,384]{4,2,3,1,0:T(8,128)(2,1)}, u32[]{:S(2)}, u32[]{:S(2)}) async-start(bf16[4,4,32,4,384]{4,2,3,1,0:T(8,128)(2,1)} %pad_maximum_fusion), calls=%async_computation | async-start | bytes 3145728 | tf_op jit(solution)/shard_map/all_to_all | solution.py:24
  34.8 28.9 %all-to-all-done = bf16[4,4,32,4,384]{4,2,3,1,0:T(8,128)(2,1)} async-done(((bf16[4,4,32,4,384]{4,2,3,1,0:T(8,128)(2,1)}), bf16[4,4,32,4,384]{4,2,3,1,0:T(8,128)(2,1)}, u32[]{:S(2)}, u32[]{:S(2)}) %all-to-all-start) | async-done | bytes 1572896 | tf_op jit(solution)/shard_map/all_to_all | solution.py:24
  63.7 4.4 all-to-all-start.2
  70.9 6.0 %fusion.34 = f32[4,384,2048]{2,1,0:T(8,128)S(1)} fusion(bf16[512,4,384]{2,0,1:T(8,128)(2,1)S(1)} %bitcast.140, bf16[4,512,2048]{2,1,0:T(8,128)(2,1)} %param.8), kind=kOutput, calls=%fused_computation.65 | convolution fusion | flops 3221225472 | bytes 22544384 | tf_op jit(solution)/shard_map/mjt,jmo->jot/dot_general | solution.py:50
  76.8 11.5 %fusion.33 = f32[4,384,512]{1,2,0:S(1)} fusion(bf16[4,2048,512]{2,1,0:T(8,128)(2,1)} %param.9, f32[4,384,2048]{2,1,0:T(8,128)S(1)} %fusion.34), kind=kOutput, calls=%fused_computation.64 | convolution fusion | flops 3249537024 | bytes 24117248
  90.1 14.5 %all-to-all-done.2 = bf16[4,4,32,4,384]{4,2,3,1,0:T(8,128)(2,1)} async-done(((bf16[4,4,32,4,384]{4,2,3,1,0:T(8,128)(2,1)}), bf16[4,4,32,4,384]{4,2,3,1,0:T(8,128)(2,1)}, u32[]{:S(2)}, u32[]{:S(2)}) %all-to-all-start.2) | async-done | bytes 1572896 | tf_op jit(solution)/shard_map/all_to_all | solution.py:24
  104.6 4.4 all-to-all-start.1
  112.3 17.6 %fusion.6 = bf16[4,2048,384]{1,2,0:T(8,128)(2,1)} fusion(f32[4,384,2048]{2,1,0:T(8,128)} %copy-done.1, bf16[512,4,384]{2,0,1:T(8,128)(2,1)S(1)} %bitcast.144, bf16[4,2048,512]{2,1,0:T(8,128)(2,1)} %param.9), kind=kOutput, calls=%fused_computation.10 | convolution fusion | flops 3280994304 | bytes 28835840 | tf_op jit(solution)/shard_map/ojt,jmo->jmt/dot_general | solution.py:81
  129.9 15.5 %all-to-all-done.1 = bf16[4,4,32,4,384]{4,2,3,1,0:T(8,128)(2,1)} async-done(((bf16[4,4,32,4,384]{4,2,3,1,0:T(8,128)(2,1)}), bf16[4,4,32,4,384]{4,2,3,1,0:T(8,128)(2,1)}, u32[]{:S(2)}, u32[]{:S(2)}) %all-to-all-start.1) | async-done | bytes 1572896 | tf_op jit(solution)/shard_map/all_to_all | solution.py:24
  150.9 9.9 %fusion.24 = bf16[4,32,16,384]{3,1,2,0:T(8,128)(2,1)S(1)} fusion(bf16[4,16,32,2048]{3,2,1,0:T(8,128)(2,1)} %bitcast.133, bf16[4,2048,384]{1,2,0:T(8,128)(2,1)} %fusion.6), kind=kOutput, calls=%fused_computation.43 | convolution fusion | flops 3222011904 | bytes 16252928 | tf_op jit(solution)/shard_map/jot,jbco->jcbt/dot_general | solution.py:93
  162.4 4.4 all-to-all-start.3
  167.0 11.5 %fusion.7 = bf16[512,4,2048]{0,2,1:T(8,128)(2,1)} fusion(bf16[4,2048,384]{1,2,0:T(8,128)(2,1)} %fusion.6, bf16[512,4,384]{2,0,1:T(8,128)(2,1)} %bitcast.141), kind=kOutput, calls=%fused_computation.13 | convolution fusion | flops 3229614080 | bytes 16252928 | tf_op jit(solution)/shard_map/mjt,jot->mjo/dot_general | solution.py:107
  178.5 14.9 %copy.77 = bf16[512,4,2048]{2,1,0:T(4,128)(2,1)} copy(bf16[512,4,2048]{0,2,1:T(8,128)(2,1)} %fusion.7) | data formatting | bytes 16777216 | tf_op jit(solution)/shard_map/convert_element_type | solution.py:118
  193.4 9.7 %all-to-all-done.3 = bf16[4,4,32,4,384]{4,2,3,1,0:T(8,128)(2,1)} async-done(((bf16[4,4,32,4,384]{4,2,3,1,0:T(8,128)(2,1)}), bf16[4,4,32,4,384]{4,2,3,1,0:T(8,128)(2,1)}, u32[]{:S(2)}, u32[]{:S(2)}) %all-to-all-start.3) | async-done | bytes 1572896 | tf_op jit(solution)/shard_map/all_to_all | solution.py:24
  208.6 4.5 copy.75
  213.3 10.9 %fusion.8 = bf16[2048,4,512]{0,2,1:T(8,128)(2,1)} fusion(bf16[512,4,384]{2,0,1:T(8,128)(2,1)} %bitcast.145, f32[4,384,2048]{2,1,0:T(8,128)} %copy-done.1), kind=kOutput, calls=%fused_computation.14 | convolution fusion | flops 3257925632 | bytes 22544384 | tf_op jit(solution)/shard_map/jmt,ojt->mjo/dot_general | solution.py:89
  230.7 4.1 convolution_bitcast_fusion.1
  238.4 4.1 fusion.12
  245.3 4.9 %convolution_bitcast_fusion = f32[384,4,512]{2,0,1:T(8,128)} fusion(bf16[512,4,384]{2,0,1:T(8,128)(2,1)} %bitcast.139, bf16[4,512,512]{2,1,0:T(8,128)(2,1)} %param.7), kind=kOutput, calls=%fused_computation.25 | convolution fusion | flops 805306368 | bytes 6815744 | tf_op jit(solution)/shard_map/obt,bio->bit/dot_general | solution.py:101
  253.8 3.9 fusion.11
  262.2 99.8 %all-reduce.5.cloned.1.call-done = (bf16[512,4,512]{2,1,0:T(4,128)(2,1)}, bf16[512,4,2048]{2,1,0:T(4,128)(2,1)}) async-done(((bf16[512,4,512]{2,1,0:T(4,128)(2,1)}, bf16[512,4,2048]{2,1,0:T(4,128)(2,1)}), (bf16[512,4,512]{2,1,0:T(4,128)(2,1)}, bf16[512,4,2048]{2,1,0:T(4,128)(2,1)})) %all-reduce.5.cloned.1.call-update) | async-done | bytes 10485776
  368.0 69.0 %reduce-scatter.3.cloned.1.call-done = bf16[256,4,512]{0,2,1:T(8,128)(2,1)} async-done(((bf16[2048,4,512]{0,2,1:T(8,128)(2,1)}), bf16[256,4,512]{0,2,1:T(8,128)(2,1)}) %reduce-scatter.3.cloned.1.call-update) | async-done | bytes 1048592 | tf_op jit(solution)/shard_map/reduce_scatter | solution.py:120
  (57 shorter events, 65.7 us)
Async XLA Ops:
  7.2 23.3 %copy-start = (bf16[4,512,512]{2,1,0:T(8,128)(2,1)S(1)}, bf16[4,512,512]{2,1,0:T(8,128)(2,1)}, u32[]{:S(2)}) copy-start(bf16[4,512,512]{2,1,0:T(8,128)(2,1)} %param.10) | copy-start | bytes 6291460
  20.3 43.4 %all-to-all-start = ((bf16[4,4,32,4,384]{4,2,3,1,0:T(8,128)(2,1)}), bf16[4,4,32,4,384]{4,2,3,1,0:T(8,128)(2,1)}, u32[]{:S(2)}, u32[]{:S(2)}) async-start(bf16[4,4,32,4,384]{4,2,3,1,0:T(8,128)(2,1)} %pad_maximum_fusion), calls=%async_computation | async-start | bytes 3145728 | tf_op jit(solution)/shard_map/all_to_all | solution.py:24
  63.7 40.9 %all-to-all-start.2 = ((bf16[4,4,32,4,384]{4,2,3,1,0:T(8,128)(2,1)}), bf16[4,4,32,4,384]{4,2,3,1,0:T(8,128)(2,1)}, u32[]{:S(2)}, u32[]{:S(2)}) async-start(bf16[4,4,32,4,384]{4,2,3,1,0:T(8,128)(2,1)} %pad_maximum_fusion.2), calls=%async_computation.2 | async-start | bytes 3145728 | tf_op jit(solution)/shard_map/all_to_all | solution.py:24
  69.7 1.1 copy-start.6
  76.8 11.5 %copy-start.1 = (f32[4,384,2048]{2,1,0:T(8,128)}, f32[4,384,2048]{2,1,0:T(8,128)S(1)}, u32[]{:S(2)}) copy-start(f32[4,384,2048]{2,1,0:T(8,128)S(1)} %fusion.34) | copy-start | bytes 37748740
  104.6 40.9 %all-to-all-start.1 = ((bf16[4,4,32,4,384]{4,2,3,1,0:T(8,128)(2,1)}), bf16[4,4,32,4,384]{4,2,3,1,0:T(8,128)(2,1)}, u32[]{:S(2)}, u32[]{:S(2)}) async-start(bf16[4,4,32,4,384]{4,2,3,1,0:T(8,128)(2,1)} %pad_maximum_fusion.1), calls=%async_computation.1 | async-start | bytes 3145728 | tf_op jit(solution)/shard_map/all_to_all | solution.py:24
  108.9 151.5 %reduce-scatter.5.cloned.1.call-start = ((), (), s32[]{:S(2)}) async-start(), calls=%async_computation.7 | async-start | bytes 2359296 | tf_op jit(solution)/shard_map/reduce_scatter | solution.py:123
  111.1 1.2 copy-start.7
  145.4 2.9 copy-start.3
  147.2 1.1 copy-start.4
  162.4 40.7 %all-to-all-start.3 = ((bf16[4,4,32,4,384]{4,2,3,1,0:T(8,128)(2,1)}), bf16[4,4,32,4,384]{4,2,3,1,0:T(8,128)(2,1)}, u32[]{:S(2)}, u32[]{:S(2)}) async-start(bf16[4,4,32,4,384]{4,2,3,1,0:T(8,128)(2,1)} %pad_maximum_fusion.3), calls=%async_computation.3 | async-start | bytes 3145728 | tf_op jit(solution)/shard_map/all_to_all | solution.py:24
  166.7 195.3 %all-reduce.5.cloned.1.call-start = ((), (), s32[]{:S(2)}) async-start(), calls=%async_computation.8 | async-start | bytes 20971520
  203.1 2.9 copy-start.2
  204.9 1.1 copy-start.5
  213.1 223.9 %reduce-scatter.3.cloned.1.call-start = ((), (), s32[]{:S(2)}) async-start(), calls=%async_computation.6 | async-start | bytes 9437184 | tf_op jit(solution)/shard_map/reduce_scatter | solution.py:120
  226.9 2.6 copy-start.8
Sparse Core Ops, SparseCore 0:
  151.1 40.3 reduce-scatter.4
  213.2 148.8 all-reduce.4
  365.5 71.3 reduce-scatter.2
